TPU v7x, 32 devices: a whole 2x2x4 slice. The times are simulated.
32 devices in a mesh: dp: 8 (over z, core), vocab: 4 (over y, x).
Axes of the slice: x: 2, y: 2, z: 4, core: 2. Of those that a mesh axis runs over, the one named last changes fastest.
Arguments:
- hidden: float32 [16, 2, 32, 4096], P('dp', None, None, 'vocab'), may hold values from -64 to 64, as said below
- head_weight: float32 [4096, 1024], P(None, 'vocab'), may hold values from -1 to 1, as said below
- targets: int32 [16, 2, 32], P('dp'), may hold values from 0 to 1023
- lengths: int32 [16, 2], P('dp'), may hold values from 8 to 32
- rest_lse: float32 [16, 2, 32], P('dp'), may hold values from 6 to 10
- ref_logp: float32 [16, 2], P('dp'), may hold values from -120 to 120
- group_map: int32 [16], P('dp'), may hold values from 0 to 7, as said below
- group_weight: float32 [8], replicated, may hold values from 0.25 to 4
Outputs:
- hidden_grad: float32 [16, 2, 32, 4096], P('dp', None, None, 'vocab')
- dpo_loss: float32 [], replicated
Inputs may be any that keep to these rules, and one draw needn't show every extreme that they name: `hidden`: standard normal states; in some draws a few tokens lie near large multiples of two head columns. `head_weight`: entries of order one over the square root of 4096. `group_map`: each pair names its own group or one of the two next to it (indices modulo 8); every group is named by exactly 2 pairs, and at most one pair of a group names each neighbour.
All inputs are finite; a program needn't handle non-finite values.
Results may differ from a plain program's by a relative error of at most 0.0003.
Values sent between devices are 32-bit elements; how exact they have to be, the bound alone decides.
A program may use at most 64 MiB of HBM per device.

v0:
```python
import jax
import jax.numpy as jnp
from jax import lax
from jax.sharding import PartitionSpec as P

beta_scale = 0.05
highest = lax.Precision.HIGHEST


def shards(hidden, head_weight, targets, lengths, rest_lse, ref_logp, group_map, group_weight):
    pair_count = hidden.shape[0]
    seq_slots = hidden.shape[2]
    local_width = hidden.shape[3]
    column_count = head_weight.shape[1]
    group_count = group_weight.shape[0]
    group_ids = lax.iota(jnp.int32, group_count)
    pair_weight = jnp.sum(
        jnp.where(group_map[:, None] == group_ids[None, :], group_weight[None, :], 0.0), axis=1
    )
    token_count = pair_count * 2 * seq_slots
    state_rows = hidden.reshape(token_count, local_width)
    vocab_index = lax.axis_index("vocab")
    column_ids = vocab_index * column_count + lax.iota(jnp.int32, column_count)
    matches = targets.reshape(token_count)[:, None] == column_ids[None, :]
    logits = jnp.dot(
        lax.all_gather(state_rows, "vocab", axis=1, tiled=True),
        head_weight,
        precision=highest,
        preferred_element_type=jnp.float32,
    )
    local_peak = jnp.max(logits, axis=1)
    local_total = jnp.sum(jnp.exp(logits - local_peak[:, None]), axis=1)
    local_target = jnp.sum(jnp.where(matches, logits, 0.0), axis=1)
    row_peak = lax.pmax(local_peak, "vocab")
    row_total, target_logit = lax.psum(
        (local_total * jnp.exp(local_peak - row_peak), local_target), "vocab"
    )
    window_lse = row_peak + jnp.log(row_total)
    outside = rest_lse.reshape(token_count)
    ceiling = jnp.maximum(window_lse, outside)
    full_lse = ceiling + jnp.log(jnp.exp(window_lse - ceiling) + jnp.exp(outside - ceiling))
    positions = lax.iota(jnp.int32, seq_slots)
    live_tokens = (positions[None, None, :] < lengths[:, :, None]).astype(jnp.float32)
    token_logp = (target_logit - full_lse).reshape(pair_count, 2, seq_slots) * live_tokens
    sequence_logp = jnp.sum(token_logp, axis=2)
    margin = beta_scale * (
        sequence_logp[:, 0] - ref_logp[:, 0] - (sequence_logp[:, 1] - ref_logp[:, 1])
    )
    divisor = pair_count * jnp.sum(group_weight)
    local_loss = jnp.sum(pair_weight * jax.nn.softplus(-margin)) / divisor
    dpo_loss = lax.psum(local_loss, "dp")
    coefficient = -beta_scale * pair_weight * jax.nn.sigmoid(-margin) / divisor
    sign_pair = jnp.array([1.0, -1.0], jnp.float32)
    token_grad = (coefficient[:, None, None] * sign_pair[None, :, None] * live_tokens).reshape(
        token_count
    )
    probability = jnp.exp(logits - full_lse[:, None])
    logit_grad = token_grad[:, None] * (matches.astype(jnp.float32) - probability)
    partial_grad = jnp.dot(
        logit_grad, head_weight.T, precision=highest, preferred_element_type=jnp.float32
    )
    grad_rows = lax.psum_scatter(partial_grad, "vocab", scatter_dimension=1, tiled=True)
    hidden_grad = grad_rows.reshape(pair_count, 2, seq_slots, local_width)
    return (hidden_grad, dpo_loss)


def solution(mesh):
    return jax.shard_map(
        shards,
        mesh=mesh,
        in_specs=(
            P("dp", None, None, "vocab"),
            P(None, "vocab"),
            P("dp", None, None),
            P("dp", None),
            P("dp", None, None),
            P("dp", None),
            P("dp"),
            P(),
        ),
        out_specs=(P("dp", None, None, "vocab"), P()),
        check_vma=False,
    )
```

profile of v0, /device:TPU:0, one launch (start us, length us, event | category | flops | bytes accessed | tf_op | source)
XLA Modules:
  0.0 122.3 jit_solution(11991229094027899787)
XLA Ops:
  7.2 0.0 copy-start.2
  7.2 0.0 all-gather.2.cloned.1.call-start
  7.2 0.7 all-gather.2.cloned.1.call-update
  7.9 0.0 reduce-scatter.2.cloned.1.call-start
  8.0 0.8 eq.31
  8.7 0.8 reshape.116
  9.5 1.3 %reduce_sum.58 = f32[]{:T(128)} reduce(f32[8]{0:T(128)} %param.16, f32[]{:T(128)} %constant.9.clone.1), dimensions={0}, to_apply=%region_8.9 | reduce | flops 7 | bytes 40 | tf_op jit(solution)/shard_map/reduce_sum | solution.py:49
  11.4 0.9 fusion.12
  12.3 35.5 %all-gather.2.cloned.1.call-done = f32[128,4096]{1,0:T(8,128)} async-done(((f32[128,1024]{1,0:T(8,128)}), f32[128,4096]{1,0:T(8,128)}) %all-gather.2.cloned.1.call-update) | async-done | bytes 2097168 | tf_op jit(solution)/shard_map/all_gather | solution.py:26
  47.8 5.0 %fusion.18 = (f32[128]{0:T(128)S(1)}, f32[128,256]{1,0:T(8,128)S(1)}) fusion(f32[128,4096]{1,0:T(8,128)} %all-gather.2.cloned.1.call-done, f32[4096,256]{1,0:T(8,128)} %param.10), kind=kOutput, calls=%fused_computation.33 | convolution fusion | flops 1610645376 | bytes 6423040 | tf_op jit(solution)/shard_map/dot_general | solution.py:25
  52.8 8.9 %pmax.7 = f32[128]{0:T(128)S(1)} all-reduce(f32[128]{0:T(128)S(1)} %get-tuple-element.12), channel_id=1, replica_groups=mesh['dp'=8,'vocab'=4] {'vocab'}, use_global_device_ids=true, to_apply=%region_4.5 | all-reduce | flops 128 | bytes 1024 | tf_op jit(solution)/shard_map/pmax | solution.py:34
  61.7 0.2 fusion
  61.9 8.9 %all-reduce = (f32[128]{0:T(128)S(1)}, f32[128]{0:T(128)S(1)}) all-reduce(f32[128]{0:T(128)S(1)} %exponential_multiply_fusion, f32[128]{0:T(128)S(1)} %get-tuple-element.2), channel_id=1, replica_groups=mesh['dp'=8,'vocab'=4] {'vocab'}, use_global_device_ids=true, to_apply=%region_6.7 | all-reduce | flops 256 | bytes 2048 | tf_op jit(solution)/shard_map/psum | solution.py:35
  70.8 0.1 reshape.117
  70.9 0.2 select_reduce_fusion
  71.1 0.2 negate_reduce_fusion
  71.3 0.6 fusion.16
  71.9 0.1 broadcast_multiply_fusion
  72.0 0.1 fusion.11
  72.1 0.1 mul.81
  72.2 7.9 %fusion.3 = f32[128,4096]{1,0:T(8,128)} fusion(f32[4096,256]{1,0:T(8,128)} %param.10, f32[128,256]{1,0:T(8,128)S(1)} %get-tuple-element.13, f32[128]{0:T(128)S(1)} %get-tuple-element.9, f32[128]{0:T(128)S(1)} %mul.81, s32[256]{0:T(256)S(1)} %iota_add_fusion, s32[128]{0:T(128)S(1)} %eq.31), kind=kOutput, calls=%fused_computation.5 | convolution fusion | flops 1610776576 | bytes 6425088 | tf_op jit(solution)/shard_map/dot_general | solution.py:59
  80.1 0.0 reduce-scatter.2.cloned.1.call-update
  80.8 14.1 %psum.23 = f32[]{:T(128)} all-reduce(f32[]{:T(128)S(6)} %div.23), channel_id=1, replica_groups=mesh['dp'=8,'vocab'=4] {'dp'}, use_global_device_ids=true, to_apply=%region_11.12 | all-reduce | flops 1 | bytes 8 | tf_op jit(solution)/shard_map/psum | solution.py:51
  94.9 20.6 %reduce-scatter.2.cloned.1.call-done = f32[128,1024]{1,0:T(8,128)} async-done(((f32[128,4096]{1,0:T(8,128)}), f32[128,1024]{1,0:T(8,128)}) %reduce-scatter.2.cloned.1.call-update) | async-done | bytes 524304 | tf_op jit(solution)/shard_map/reduce_scatter | solution.py:62
  (8 shorter events, 0.0 us)
Async XLA Ops:
  7.2 64.8 %copy-start.2 = (f32[2]{0:T(128)S(1)}, f32[2]{0:T(128)}, u32[]{:S(2)}) copy-start(f32[2]{0:T(128)} %constant.24.clone) | copy-start | bytes 28
  7.2 63.7 %copy-start.1 = (s32[2,2]{1,0:T(2,128)S(1)}, s32[2,2]{1,0:T(2,128)}, u32[]{:S(2)}) copy-start(s32[2,2]{1,0:T(2,128)} %param.12) | copy-start | bytes 52
  7.2 63.9 %copy-start = (f32[2,2]{1,0:T(2,128)S(1)}, f32[2,2]{1,0:T(2,128)}, u32[]{:S(2)}) copy-start(f32[2,2]{1,0:T(2,128)} %param.14) | copy-start | bytes 52
  7.2 40.6 %all-gather.2.cloned.1.call-start = ((), (), s32[]{:S(2)}) async-start(), calls=%async_computation.1 | async-start | bytes 2621440 | tf_op jit(solution)/shard_map/all_gather | solution.py:26
  7.9 107.5 %reduce-scatter.2.cloned.1.call-start = ((), (), s32[]{:S(2)}) async-start(), calls=%async_computation.2 | async-start | bytes 2621440 | tf_op jit(solution)/shard_map/reduce_scatter | solution.py:62
Sparse Core Ops, SparseCore 0:
  9.8 37.8 all-gather.1
  80.2 35.1 reduce-scatter.1
where the time goes:
time: 123 us; the launch traced here: 122 us
  waiting for transfers between devices  56.8 us (46%)
  blocking collectives  31.9 us (26%)
  between operations  15.4 us (13%)
  matrix products  12.9 us (10%)
  other arithmetic  3.49 us (3%)
  local copies, waits for them, and re-layouts  1.71 us (1%)
    all_gather x1, waiting for transfers between devices, shards(): lax.all_gather(state_rows, 'vocab', axis=1, tiled=True)  35.5 us
    reduce_scatter x1, waiting for transfers between devices, shards(): lax.psum_scatter(partial_grad, 'vocab', scatter_dimension=1, tiled=True)  20.6 us
    psum x1, blocking collectives, shards(): dpo_loss = lax.psum(local_loss, 'dp')  14.1 us
    pmax x1, blocking collectives, shards(): row_peak = lax.pmax(local_peak, 'vocab')  8.94 us
    psum x1, blocking collectives, shards(): lax.psum((local_total * jnp.exp(local_peak - row_peak), local_target), 'v...  8.88 us
    dot_general x1, matrix products, shards(): jnp.dot(logit_grad, head_weight.T, precision=highest, preferred_element_t...  7.94 us
    dot_general x1, matrix products, shards(): jnp.dot(lax.all_gather(state_rows, 'vocab', axis=1, tiled=True), head_wei...  4.99 us
  transfers between devices with their start and end apart: 2, of which 2 were waited for; matrix products, arithmetic and copies ran while one was open for 3% of the time, Pallas kernels for 0%

commit v1 on v0

v1 whole, which is shorter than its diff:
```python
import functools

import jax
import jax.numpy as jnp
from jax import lax
from jax.experimental import pallas as pl
from jax.experimental.pallas import tpu as pltpu
from jax.sharding import PartitionSpec as P

beta_scale = 0.05
SHARE = 4
CHUNKS = 2
MESH = pl.DeviceIdType.MESH
f32, bf16 = jnp.float32, jnp.bfloat16
LANES = 128


def split(x):
    high = x.astype(bf16)
    return high, (x - high.astype(f32)).astype(bf16)


def kernel(n, m, hid, w, tgt, lens, rest, refl, gmap, gw, out, loss,
           hbuf, h2, wbuf, whi, wlo, plog, rbuf, gbuf, stat, lbuf,
           lsem, wsend, wrecv, zsend, zrecv, csend, crecv, rsend, rrecv, gsend, grecv, ssend, srecv, dsend, drecv):
    v, d = lax.axis_index("vocab"), lax.axis_index("dp")
    pairs, _, seq = tgt.shape
    tokens, rows = hid.shape
    cols = w.shape[1]
    groups = gw.shape[0]
    mine = tokens // n
    quarter = rows // SHARE
    chunk = quarter // CHUNKS
    share = d % SHARE
    partner = {"dp": d + 1 - 2 * (d % 2)}
    across = {"dp": d + 2 - 4 * ((d // 2) % 2)}
    across_share = (share + 2) % SHARE

    def peer(i):
        u, bit = v, 1
        while bit <= i:
            if i & bit:
                u = u + bit * (1 - 2 * ((v // bit) % 2))
            bit *= 2
        return u

    peers = [peer(i) for i in range(n)]

    def remote(src, dst, ss, rs, where):
        return pltpu.make_async_remote_copy(
            src_ref=src, dst_ref=dst, send_sem=ss, recv_sem=rs, device_id=where, device_id_type=MESH
        )

    barrier = pltpu.get_barrier_semaphore()
    for i in range(1, n):
        pl.semaphore_signal(barrier, inc=1, device_id={"vocab": peers[i]}, device_id_type=MESH)
    for j in range(1, m):
        pl.semaphore_signal(barrier, inc=1, device_id={"dp": (d + j) % m}, device_id_type=MESH)
    own_w = pltpu.make_async_copy(w.at[pl.ds(pl.multiple_of(v * rows, rows), rows), :], wbuf.at[v], lsem.at[0])
    own_h = pltpu.make_async_copy(hid, hbuf, lsem.at[1])
    own_w.start()
    own_h.start()
    pl.semaphore_wait(barrier, n + m - 2)

    order = sorted(
        ((i, c) for i in range(1, n) for c in range(CHUNKS)), key=lambda e: (bin(e[0]).count("1"), e[1], e[0])
    )

    def spot(part, c):
        return pl.ds(pl.multiple_of(part * quarter + c * chunk, chunk), chunk)

    def plane(i, c):
        start = pl.multiple_of(peers[i] * rows + share * quarter + c * chunk, chunk)
        return remote(w.at[pl.ds(start, chunk), :], wbuf.at[v, spot(share, c)],
                      wsend.at[i - 1, c], wrecv.at[i - 1, c], {"vocab": peers[i]})

    def along(i, c):
        here = wbuf.at[peers[i], spot(share, c)]
        return remote(here, here, zsend.at[i - 1, c], zrecv.at[i - 1, c], across)

    def beside(kind, i, c):
        here = wbuf.at[peers[i], spot(across_share if kind else share, c)]
        return remote(here, here, csend.at[kind, i - 1, c], crecv.at[kind, i - 1, c], partner)

    for i, c in order:
        plane(i, c).start()

    own_h.wait()
    high, low = split(hbuf[...])
    h2[pl.ds(0, tokens), :] = high
    h2[pl.ds(tokens, tokens), :] = low
    own_w.wait()

    def piece(u, i):
        return remote(plog.at[u, pl.ds(pl.multiple_of(peers[i] * mine, mine), mine), :], rbuf.at[i - 1, u],
                      rsend.at[i - 1], rrecv.at[i - 1], {"vocab": peers[i]})

    def forward(u):
        w_high, w_low = split(wbuf[u])
        whi[u] = w_high
        wlo[u] = w_low
        both = jnp.dot(h2[...], w_high, preferred_element_type=f32)
        rest_part = jnp.dot(h2[pl.ds(0, tokens), :], w_low, preferred_element_type=f32)
        plog[u] = both[:tokens] + both[tokens:] + rest_part
        for i in range(1, n):
            piece(u, i).start()

    forward(v)

    lag = 2
    waited = []
    total = len(order)
    for k in range(total + 2 * lag):
        if k < total:
            i, c = order[k]
            plane(i, c).wait_recv()
            along(i, c).start()
            beside(0, i, c).start()
        if lag <= k < total + lag:
            i, c = order[k - lag]
            along(i, c).wait_recv()
            beside(1, i, c).start()
        if k >= 2 * lag:
            i, c = order[k - 2 * lag]
            beside(0, i, c).wait_recv()
            beside(1, i, c).wait_recv()
            waited.append(i)
            if waited.count(i) == CHUNKS:
                forward(peers[i])

    token = v * mine + lax.broadcasted_iota(jnp.int32, (mine, 1), 0)
    lane_seq = lax.broadcasted_iota(jnp.int32, (mine, seq), 1)

    def column(ref):
        picked = jnp.zeros((mine, seq), f32)
        for p in range(pairs):
            for s in range(2):
                row = jnp.broadcast_to(ref[p, pl.ds(s, 1), :].astype(f32), (mine, seq))
                picked = jnp.where((token // seq == 2 * p + s) & (token % seq == lane_seq), row, picked)
        return jnp.sum(picked, axis=1, keepdims=True)

    target = column(tgt).astype(jnp.int32)
    outside = column(rest)
    length = jnp.zeros((mine, 1), jnp.int32)
    for p in range(pairs):
        for s in range(2):
            length = jnp.where(token // seq == 2 * p + s, lens[p, s], length)
    live = (token % seq < length).astype(f32)
    lane = lax.broadcasted_iota(jnp.int32, (mine, cols), 1)

    for i in range(1, n):
        remote(rbuf.at[i - 1], rbuf.at[i - 1], rsend.at[i - 1], rrecv.at[i - 1], {"vocab": peers[i]}).wait_recv()
    logits = []
    for u in range(n):
        block = plog[u, pl.ds(pl.multiple_of(v * mine, mine), mine), :]
        for i in range(1, n):
            block = block + rbuf[i - 1, u]
        logits.append(block)
    peak = functools.reduce(jnp.maximum, [jnp.max(b, axis=1, keepdims=True) for b in logits])
    row_total = sum(jnp.sum(jnp.exp(b - peak), axis=1, keepdims=True) for b in logits)
    matches = [target == u * cols + lane for u in range(n)]
    target_logit = sum(
        jnp.sum(jnp.where(k, b, 0.0), axis=1, keepdims=True) for k, b in zip(matches, logits)
    )
    window_lse = peak + jnp.log(row_total)
    ceiling = jnp.maximum(window_lse, outside)
    full_lse = ceiling + jnp.log(jnp.exp(window_lse - ceiling) + jnp.exp(outside - ceiling))
    stat[v] = jnp.broadcast_to((target_logit - full_lse) * live, (mine, LANES))
    for u in range(n):
        gbuf[u, v] = matches[u].astype(f32) - jnp.exp(logits[u] - full_lse)

    def share_stat(i):
        return remote(stat.at[v], stat.at[v], ssend.at[i - 1], srecv.at[i - 1], {"vocab": peers[i]})

    def share_grad(u, i):
        return remote(gbuf.at[u, v], gbuf.at[u, v], gsend.at[u, i - 1], grecv.at[u, i - 1], {"vocab": peers[i]})

    for i in range(1, n):
        share_stat(i).start()
    for u in range(n):
        for i in range(1, n):
            share_grad(u, i).start()

    for i in range(1, n):
        share_stat(i).wait_recv()
    divisor = pairs * sum(gw[g] for g in range(groups))
    position = lax.broadcasted_iota(jnp.int32, (seq, LANES), 0)
    per_token = stat[...].reshape(tokens, LANES)
    local_loss = jnp.zeros((1, LANES), f32)
    scales = []
    for p in range(pairs):
        weight = sum(jnp.where(gmap[p] == g, gw[g], 0.0) for g in range(groups))
        logp = [
            jnp.sum(per_token[(2 * p + s) * seq:(2 * p + s + 1) * seq], axis=0, keepdims=True) for s in range(2)
        ]
        margin = beta_scale * ((logp[0] - refl[p, 0]) - (logp[1] - refl[p, 1]))
        softplus = jnp.maximum(-margin, 0.0) + jnp.log1p(jnp.exp(-jnp.abs(margin)))
        local_loss = local_loss + weight * softplus
        falling = jnp.exp(-jnp.abs(margin))
        sigmoid = jnp.where(margin > 0.0, falling, 1.0) / (1.0 + falling)
        coefficient = -beta_scale * weight * sigmoid / jnp.full((1, LANES), divisor)
        for s in range(2):
            signed = coefficient if s == 0 else -coefficient
            scales.append(jnp.where(position < lens[p, s], jnp.broadcast_to(signed, (seq, LANES)), 0.0))
    lbuf[d] = jnp.broadcast_to(local_loss / jnp.full((1, LANES), divisor), (8, LANES))

    def share_loss(j):
        return remote(lbuf.at[d], lbuf.at[d], dsend, drecv, {"dp": (d + j) % m})

    for j in range(1, m):
        share_loss(j).start()

    contract = (((1,), (1,)), ((), ()))
    for u in range(n):
        for i in range(1, n):
            share_grad(u, i).wait_recv()
        high, low = split(gbuf[u].reshape(tokens, cols))
        part = lax.dot_general(jnp.concatenate([high, low], axis=0), whi[u], contract, preferred_element_type=f32)
        part = part[:tokens] + part[tokens:] + lax.dot_general(high, wlo[u], contract, preferred_element_type=f32)
        if u:
            part = part + out[...]
        if u == n - 1:
            part = part * jnp.concatenate(scales, axis=0)[:, :1]
        out[...] = part

    every_loss = remote(lbuf.at[pl.ds(0, m - 1)], lbuf.at[pl.ds(0, m - 1)], dsend, drecv, partner)
    every_loss.wait_recv()
    summed = lbuf[0]
    for j in range(1, m):
        summed = summed + lbuf[j]
    loss[0, 0] = summed[0, 0]

    for i, c in order:
        plane(i, c).wait_send()
        along(i, c).wait_send()
        beside(0, i, c).wait_send()
        beside(1, i, c).wait_send()
    for i in range(1, n):
        remote(rbuf.at[i - 1], rbuf.at[i - 1], rsend.at[i - 1], rrecv.at[i - 1], {"vocab": peers[i]}).wait_send()
        share_stat(i).wait_send()
        for u in range(n):
            share_grad(u, i).wait_send()
    every_loss.wait_send()


def solution(mesh):
    n, m = mesh.shape["vocab"], mesh.shape["dp"]

    def shards(hidden, head_weight, targets, lengths, rest_lse, ref_logp, group_map, group_weight):
        rows = hidden.shape[3]
        tokens = hidden.shape[0] * hidden.shape[1] * hidden.shape[2]
        cols = head_weight.shape[1]
        mine = tokens // n
        vmem, smem = pl.BlockSpec(memory_space=pltpu.VMEM), pl.BlockSpec(memory_space=pltpu.SMEM)
        hbm = pl.BlockSpec(memory_space=pl.ANY)
        dma = pltpu.SemaphoreType.DMA
        grad, loss = pl.pallas_call(
            functools.partial(kernel, n, m),
            out_shape=(jax.ShapeDtypeStruct((tokens, rows), f32), jax.ShapeDtypeStruct((1, 1), f32)),
            in_specs=[hbm, hbm, vmem, smem, vmem, smem, smem, smem],
            out_specs=(vmem, smem),
            scratch_shapes=[
                pltpu.VMEM((tokens, rows), f32),
                pltpu.VMEM((2 * tokens, rows), bf16),
                pltpu.VMEM((n, rows, cols), f32),
                pltpu.VMEM((n, rows, cols), bf16),
                pltpu.VMEM((n, rows, cols), bf16),
                pltpu.VMEM((n, tokens, cols), f32),
                pltpu.VMEM((n - 1, n, mine, cols), f32),
                pltpu.VMEM((n, n, mine, cols), f32),
                pltpu.VMEM((n, mine, LANES), f32),
                pltpu.VMEM((m, 8, LANES), f32),
                dma((2,)),
                dma((n - 1, CHUNKS)), dma((n - 1, CHUNKS)),
                dma((n - 1, CHUNKS)), dma((n - 1, CHUNKS)),
                dma((2, n - 1, CHUNKS)), dma((2, n - 1, CHUNKS)),
                dma((n - 1,)), dma((n - 1,)),
                dma((n, n - 1)), dma((n, n - 1)),
                dma((n - 1,)), dma((n - 1,)),
                dma, dma,
            ],
            compiler_params=pltpu.CompilerParams(
                collective_id=0, has_side_effects=True, vmem_limit_bytes=56 << 20
            ),
        )(hidden.reshape(tokens, rows), head_weight, targets, lengths, rest_lse, ref_logp, group_map, group_weight)
        return grad.reshape(hidden.shape), loss.reshape(())

    return jax.shard_map(
        shards,
        mesh=mesh,
        in_specs=(
            P("dp", None, None, "vocab"),
            P(None, "vocab"),
            P("dp", None, None),
            P("dp", None),
            P("dp", None, None),
            P("dp", None),
            P("dp"),
            P(),
        ),
        out_specs=(P("dp", None, None, "vocab"), P()),
        check_vma=False,
    )
```

time: 123 us -> 50.5 us (0.41)
  waiting for transfers between devices: 56.8 us -> 0 us
  Pallas kernels: 0 us -> 46.1 us
  blocking collectives: 31.9 us -> 0 us
  between operations: 15.4 us -> 2.34 us
  matrix products: 12.9 us -> 0 us
  other arithmetic: 3.49 us -> 0 us
    pallas_call x0 -> x1, Pallas kernels: none -> 46.1 us  [shards(): pl.pallas_call(functools.partial(kernel, n, m), out_shape=(jax.ShapeDtype...]
    all_gather x1 -> x0, waiting for transfers between devices: 35.5 us -> none  [shards(): lax.all_gather(state_rows, 'vocab', axis=1, tiled=True)]
    psum x2 -> x0, blocking collectives: 23 us -> none  [the longest x1 14.1 us: shards(): dpo_loss = lax.psum(local_loss, 'dp')]
    reduce_scatter x1 -> x0, waiting for transfers between devices: 20.6 us -> none  [shards(): lax.psum_scatter(partial_grad, 'vocab', scatter_dimension=1, tiled=True)]
    dot_general x2 -> x0, matrix products: 12.9 us -> none  [the longest x1 7.94 us: shards(): jnp.dot(logit_grad, head_weight.T, precision=highest, preferred_element_t...]
    pmax x1 -> x0, blocking collectives: 8.94 us -> none  [shards(): row_peak = lax.pmax(local_peak, 'vocab')]
    reduce_sum x5 -> x0, other arithmetic: 3.09 us -> none  [the longest x1 1.26 us: shards(): divisor = pair_count * jnp.sum(group_weight)]
    unnamed x6 -> x1, local copies, waits for them, and re-layouts: 0.02 us -> 1.89 us
  transfers between devices with their start and end apart: 2 -> 0, of which waited for: 2 -> 0; matrix products, arithmetic and copies ran while one was open for 3% -> 0% of each run, Pallas kernels for 0% -> 0%
where the time goes in v1:
time: 50.5 us; the launch traced here: 50.3 us
  Pallas kernels  46.1 us (91%)
  between operations  2.34 us (5%)
  local copies, waits for them, and re-layouts  1.89 us (4%)
    pallas_call x1, Pallas kernels, shards(): pl.pallas_call(functools.partial(kernel, n, m), out_shape=(jax.ShapeDtype...  46.1 us
    unnamed x1, local copies, waits for them, and re-layouts  1.89 us

profile of v1, /device:TPU:0, one launch (start us, length us, event | category | flops | bytes accessed | tf_op | source)
XLA Modules:
  0.0 50.3 jit_solution(14863655813202418518)
XLA Ops:
  0.6 46.1 %shard_map.95 = (f32[128,1024]{1,0:T(8,128)}, f32[1,1]{1,0:T(1,128)}) custom-call(f32[128,1024]{1,0:T(8,128)} %bitcast.4, f32[4096,256]{1,0:T(8,128)} %w.1, s32[2,2,32]{2,1,0:T(2,128)} %tgt.1, s32[2,2]{1,0:T(2,128)} %lens.1, f32[2,2,32]{2,1,0:T(2,128)} %rest.1, f32[2,2]{1,0:T(2,128)} %refl.1, s32[2]{0:T(128)} %gmap.1, f32[8]{0:T(128)} %gw.1), custom_call_target="tpu_custom_call" | custom-call | tf_op jit(solution)/shard_map/pallas_call | solution.py:257
  46.7 1.9 %copy.12 = f32[2,2,32,1024]{3,2,1,0:T(8,128)} copy(f32[2,2,32,1024]{3,2,1,0:T(8,128)} %bitcast.3) | data formatting | bytes 1048576

commit v2 on v1

--- a/solution.py
+++ b/solution.py
@@ -9,7 +9,8 @@
 
 beta_scale = 0.05
 SHARE = 4
-CHUNKS = 2
+CHUNKS = 4
+DIRECT = 2
 MESH = pl.DeviceIdType.MESH
 f32, bf16 = jnp.float32, jnp.bfloat16
 LANES = 128
@@ -62,19 +63,30 @@
     own_h.start()
     pl.semaphore_wait(barrier, n + m - 2)
 
+    def hops(i):
+        return bin(i).count("1")
+
     order = sorted(
-        ((i, c) for i in range(1, n) for c in range(CHUNKS)), key=lambda e: (bin(e[0]).count("1"), e[1], e[0])
+        ((i, c) for i in range(1, n) for c in range(CHUNKS)), key=lambda e: (e[1] - hops(e[0]), -hops(e[0]), e[0])
     )
+
+    def direct(i, c):
+        return hops(i) == 1 and c >= CHUNKS - DIRECT
 
     def spot(part, c):
         return pl.ds(pl.multiple_of(part * quarter + c * chunk, chunk), chunk)
 
-    def plane(i, c):
-        start = pl.multiple_of(peers[i] * rows + share * quarter + c * chunk, chunk)
-        return remote(w.at[pl.ds(start, chunk), :], wbuf.at[v, spot(share, c)],
-                      wsend.at[i - 1, c], wrecv.at[i - 1, c], {"vocab": peers[i]})
-
-    def along(i, c):
+    def plane(i, c, part, ss, rs):
+        start = pl.multiple_of(peers[i] * rows + part * quarter + c * chunk, chunk)
+        return remote(w.at[pl.ds(start, chunk), :], wbuf.at[v, spot(part, c)],
+                      ss.at[i - 1, c], rs.at[i - 1, c], {"vocab": peers[i]})
+
+    def first(i, c):
+        return plane(i, c, share, wsend, wrecv)
+
+    def second(i, c):
+        if direct(i, c):
+            return plane(i, c, across_share, zsend, zrecv)
         here = wbuf.at[peers[i], spot(share, c)]
         return remote(here, here, zsend.at[i - 1, c], zrecv.at[i - 1, c], across)
 
@@ -83,7 +95,9 @@
         return remote(here, here, csend.at[kind, i - 1, c], crecv.at[kind, i - 1, c], partner)
 
     for i, c in order:
-        plane(i, c).start()
+        first(i, c).start()
+        if direct(i, c):
+            second(i, c).start()
 
     own_h.wait()
     high, low = split(hbuf[...])
@@ -113,12 +127,13 @@
     for k in range(total + 2 * lag):
         if k < total:
             i, c = order[k]
-            plane(i, c).wait_recv()
-            along(i, c).start()
+            first(i, c).wait_recv()
+            if not direct(i, c):
+                second(i, c).start()
             beside(0, i, c).start()
         if lag <= k < total + lag:
             i, c = order[k - lag]
-            along(i, c).wait_recv()
+            second(i, c).wait_recv()
             beside(1, i, c).start()
         if k >= 2 * lag:
             i, c = order[k - 2 * lag]
@@ -231,8 +246,8 @@
     loss[0, 0] = summed[0, 0]
 
     for i, c in order:
-        plane(i, c).wait_send()
-        along(i, c).wait_send()
+        first(i, c).wait_send()
+        second(i, c).wait_send()
         beside(0, i, c).wait_send()
         beside(1, i, c).wait_send()
     for i in range(1, n):

time: 50.5 us -> 46.9 us (0.929)
  Pallas kernels: 46.1 us -> 42.5 us
    pallas_call x1, Pallas kernels: 46.1 us -> 42.5 us  [shards(): pl.pallas_call(functools.partial(kernel, n, m), out_shape=(jax.ShapeDtype...]
where the time goes in v2:
time: 46.9 us; the launch traced here: 46.7 us
  Pallas kernels  42.5 us (91%)
  between operations  2.34 us (5%)
  local copies, waits for them, and re-layouts  1.89 us (4%)
    pallas_call x1, Pallas kernels, shards(): pl.pallas_call(functools.partial(kernel, n, m), out_shape=(jax.ShapeDtype...  42.5 us
    unnamed x1, local copies, waits for them, and re-layouts  1.89 us

profile of v2, /device:TPU:0, one launch (start us, length us, event | category | flops | bytes accessed | tf_op | source)
XLA Modules:
  0.0 46.7 jit_solution(12755246265739994288)
XLA Ops:
  0.6 42.5 %shard_map.95 = (f32[128,1024]{1,0:T(8,128)}, f32[1,1]{1,0:T(1,128)}) custom-call(f32[128,1024]{1,0:T(8,128)} %bitcast.4, f32[4096,256]{1,0:T(8,128)} %w.1, s32[2,2,32]{2,1,0:T(2,128)} %tgt.1, s32[2,2]{1,0:T(2,128)} %lens.1, f32[2,2,32]{2,1,0:T(2,128)} %rest.1, f32[2,2]{1,0:T(2,128)} %refl.1, s32[2]{0:T(128)} %gmap.1, f32[8]{0:T(128)} %gw.1), custom_call_target="tpu_custom_call" | custom-call | tf_op jit(solution)/shard_map/pallas_call | solution.py:272
  43.1 1.9 %copy.12 = f32[2,2,32,1024]{3,2,1,0:T(8,128)} copy(f32[2,2,32,1024]{3,2,1,0:T(8,128)} %bitcast.3) | data formatting | bytes 1048576

commit v3 on v2

--- a/solution.py
+++ b/solution.py
@@ -116,7 +116,7 @@
         both = jnp.dot(h2[...], w_high, preferred_element_type=f32)
         rest_part = jnp.dot(h2[pl.ds(0, tokens), :], w_low, preferred_element_type=f32)
         plog[u] = both[:tokens] + both[tokens:] + rest_part
-        for i in range(1, n):
+        for i in reversed(range(1, n)):
             piece(u, i).start()
 
     forward(v)
@@ -193,7 +193,7 @@
     for i in range(1, n):
         share_stat(i).start()
     for u in range(n):
-        for i in range(1, n):
+        for i in reversed(range(1, n)):
             share_grad(u, i).start()
 
     for i in range(1, n):

time: 46.9 us -> 46.5 us (level)
  no operation moved by 1% of the time
where the time goes in v3:
time: 46.5 us; the launch traced here: 46.3 us
  Pallas kernels  42.1 us (91%)
  between operations  2.34 us (5%)
  local copies, waits for them, and re-layouts  1.89 us (4%)
    pallas_call x1, Pallas kernels, shards(): pl.pallas_call(functools.partial(kernel, n, m), out_shape=(jax.ShapeDtype...  42.1 us
    unnamed x1, local copies, waits for them, and re-layouts  1.89 us

profile of v3, /device:TPU:0, one launch (start us, length us, event | category | flops | bytes accessed | tf_op | source)
XLA Modules:
  0.0 46.3 jit_solution(315248299569191553)
XLA Ops:
  0.6 42.1 %shard_map.95 = (f32[128,1024]{1,0:T(8,128)}, f32[1,1]{1,0:T(1,128)}) custom-call(f32[128,1024]{1,0:T(8,128)} %bitcast.4, f32[4096,256]{1,0:T(8,128)} %w.1, s32[2,2,32]{2,1,0:T(2,128)} %tgt.1, s32[2,2]{1,0:T(2,128)} %lens.1, f32[2,2,32]{2,1,0:T(2,128)} %rest.1, f32[2,2]{1,0:T(2,128)} %refl.1, s32[2]{0:T(128)} %gmap.1, f32[8]{0:T(128)} %gw.1), custom_call_target="tpu_custom_call" | custom-call | tf_op jit(solution)/shard_map/pallas_call | solution.py:272
  42.7 1.9 %copy.12 = f32[2,2,32,1024]{3,2,1,0:T(8,128)} copy(f32[2,2,32,1024]{3,2,1,0:T(8,128)} %bitcast.3) | data formatting | bytes 1048576
